TPU v7x, 32 devices: a whole 2x2x4 slice. The times are simulated.
32 devices in a mesh: row: 8 (over y, x, core), col: 4 (over z).
Axes of the slice: x: 2, y: 2, z: 4, core: 2. Of those that a mesh axis runs over, the one named last changes fastest.
Arguments:
- panel_tiles: float32 [16384, 1024], P('row', 'col'), may hold values from -48 to 48
- left_u: bfloat16 [16384, 6144], P('row', 'col'), may hold values from -8 to 8
- earlier_right_factors: bfloat16 [16384, 6144], P('row', 'col'), may hold values from -0.25 to 0.25
- tile_global_index: int32 [16], replicated, may hold values from 0 to 15, as said below
Outputs:
- panel_factor: float32 [16384, 1024], P('row', 'col')
Inputs may be any that keep to these rules, and one draw needn't show every extreme that they name: `tile_global_index`: A permutation; slot pivot, the one numbered 0, holds the diagonal tile.
All inputs are finite; a program needn't handle non-finite values.
Results may differ from a plain program's by a relative error of at most 0.00053.
Values may be sent and summed in bfloat16 or wider, within the bound.
A program may use at most 128 MiB of HBM per device.

v0:
```python
import jax
import jax.numpy as jnp
from jax import lax
from jax.sharding import PartitionSpec as P

TILE = 1024
RANK = 256
TILE_DEV = 2
COL_DEV = 6


def from_root(value, axis, source):
    kept = jnp.where(lax.axis_index(axis) == source, value, 0).astype(value.dtype)
    return lax.psum(kept, axis)


def local(panel_tiles, left_u, earlier_right_factors, tile_global_index):
    tile_count = tile_global_index.shape[0]
    pivot_position = jnp.sum(
        jnp.where(tile_global_index == 0, jnp.arange(tile_count, dtype=jnp.int32), 0)
    )
    owner_row = pivot_position // TILE_DEV
    local_slot = pivot_position % TILE_DEV
    my_row = lax.axis_index("row")
    my_col = lax.axis_index("col")
    col_width = panel_tiles.shape[1]
    pivot_left = lax.dynamic_slice_in_dim(left_u, local_slot * TILE, TILE, 0)
    pivot_right = lax.dynamic_slice_in_dim(earlier_right_factors, local_slot * TILE, TILE, 0)
    pivot_left, pivot_right = (
        from_root(pivot_left, "row", owner_row),
        from_root(pivot_right, "row", owner_row),
    )
    left_blocks = left_u.reshape(TILE_DEV, TILE, COL_DEV, RANK)
    right_blocks = earlier_right_factors.reshape(TILE_DEV, TILE, COL_DEV, RANK)
    pivot_triple = pivot_right.reshape(TILE, COL_DEV, RANK)
    inner_small = jnp.einsum(
        "tbjr,bjs->tjrs", right_blocks, pivot_triple, preferred_element_type=jnp.float32
    ).astype(jnp.bfloat16)
    left_small = jnp.einsum(
        "tbjr,tjrs->tbjs", left_blocks, inner_small, preferred_element_type=jnp.float32
    ).astype(jnp.bfloat16)
    update_terms = jnp.einsum(
        "nk,mk->nm",
        left_small.reshape(TILE_DEV * TILE, COL_DEV * RANK),
        pivot_left,
        preferred_element_type=jnp.float32,
    )
    placed = lax.dynamic_update_slice_in_dim(
        jnp.zeros_like(update_terms), panel_tiles, my_col * col_width, 1
    )
    updated_tiles = lax.psum(placed - update_terms, "col")
    diagonal = lax.dynamic_slice_in_dim(updated_tiles, local_slot * TILE, TILE, 0)
    identity = jnp.eye(TILE, dtype=jnp.float32)
    cholesky_factor = jnp.linalg.cholesky(diagonal)
    inverted_factor = lax.linalg.triangular_solve(
        cholesky_factor, identity, left_side=True, lower=True
    )
    rows_inv = lax.dynamic_slice_in_dim(inverted_factor, my_col * col_width, col_width, 0)
    rows_inv = from_root(rows_inv, "row", owner_row)
    solved_rows = lax.dot_general(
        updated_tiles,
        rows_inv,
        (((1,), (1,)), ((), ())),
        precision=lax.Precision.HIGHEST,
        preferred_element_type=jnp.float32,
    )
    factor_cols = lax.dynamic_slice_in_dim(cholesky_factor, my_col * col_width, col_width, 1)
    row_tiles = jnp.arange(TILE_DEV * TILE, dtype=jnp.int32) // TILE
    chosen_rows = jnp.logical_and(my_row == owner_row, row_tiles == local_slot)
    return jnp.where(chosen_rows[:, None], jnp.tile(factor_cols, (TILE_DEV, 1)), solved_rows)


def solution(mesh):
    in_specs = (P("row", "col"), P("row", "col"), P("row", "col"), P())
    out_specs = P("row", "col")
    return jax.shard_map(local, mesh=mesh, in_specs=in_specs, out_specs=out_specs, check_vma=False)
```

profile of v0, /device:TPU:0, one launch (start us, length us, event | category | flops | bytes accessed | tf_op | source)
XLA Modules:
  0.0 900.8 jit_solution(1738015696041004447)
XLA Ops:
  10.7 5.9 constant_dynamic-slice_fusion.3
  16.6 3.2 copy.24
  19.8 4.7 copy.25
  24.5 2.0 broadcast_select_fusion.1
  27.5 2.0 broadcast_select_fusion
  29.6 13.5 %reshape.127 = bf16[2,1024,6,256]{3,2,1,0:T(8,128)(2,1)} reshape(bf16[2048,1536]{1,0:T(8,128)(2,1)} %param.5) | data formatting | bytes 12582912 | tf_op jit(solution)/shard_map/reshape | solution.py:33
  43.1 13.4 %reshape.126 = bf16[2,1024,6,256]{3,2,1,0:T(8,128)(2,1)} reshape(bf16[2048,1536]{1,0:T(8,128)(2,1)} %param.6) | data formatting | bytes 12582912 | tf_op jit(solution)/shard_map/reshape | solution.py:34
  56.5 1.9 copy.9
  58.5 4.3 broadcast_in_dim.26
  64.3 72.1 %all-reduce.10.cloned.1.call-done = (bf16[1024,6,256]{0,2,1:T(8,128)(2,1)}, bf16[1024,1536]{0,1:T(8,128)(2,1)}) async-done(((bf16[1024,6,256]{0,2,1:T(8,128)(2,1)}, bf16[1024,1536]{0,1:T(8,128)(2,1)}), (bf16[1024,6,256]{0,2,1:T(8,128)(2,1)}, bf16[1024,1536]{0,1:T(8,128)(2,1)})) %all-reduce.10.cloned.1.call-update) | async-done | bytes 6291472 | tf_op jit(solution)/shard_map/psum | solution.py:14
  136.3 16.6 %convert_bitcast_fusion = bf16[2,1024,6,256]{1,3,2,0:T(8,128)(2,1)} fusion(bf16[2,1024,6,256]{3,2,1,0:T(8,128)(2,1)} %reshape.127, bf16[2,1024,6,256]{3,2,1,0:T(8,128)(2,1)} %reshape.126, bf16[1024,6,256]{0,2,1:T(8,128)(2,1)} %get-tuple-element.21), kind=kOutput, calls=%fused_computation.6 | convolution fusion | flops 3225157632 | bytes 22020096 | tf_op jit(solution)/shard_map/tbjr,tjrs->tbjs/dot_general | solution.py:39
  152.9 11.9 %copy.14 = bf16[2,1024,6,256]{1,0,3,2:T(2,128)(2,1)S(1)} copy(bf16[2,1024,6,256]{1,3,2,0:T(8,128)(2,1)} %convert_bitcast_fusion) | data formatting | bytes 12582912 | tf_op jit(solution)/shard_map/convert_element_type | solution.py:41
  164.9 2.7 copy.26
  167.5 11.9 %convolution_subtract_fusion = f32[2048,1024]{0,1:T(8,128)} fusion(f32[2048,1024]{0,1:T(8,128)} %constant_dynamic-update-slice_fusion.26, bf16[2048,1536]{0,1:T(8,128)(2,1)S(1)} %bitcast.129, bf16[1024,1536]{0,1:T(8,128)(2,1)S(1)} %copy-done.3), kind=kOutput, calls=%fused_computation.13 | convolution fusion | flops 6444548096 | bytes 26214400 | tf_op jit(solution)/shard_map/nk,mk->nm/dot_general | solution.py:42
  179.8 2.4 fusion.43
  182.3 288.3 %all-reduce.6.cloned.1.call-done = f32[2048,1024]{0,1:T(8,128)} async-done(((f32[2048,1024]{0,1:T(8,128)}), f32[2048,1024]{0,1:T(8,128)}) %all-reduce.6.cloned.1.call-update) | async-done | bytes 8388624 | tf_op jit(solution)/shard_map/psum | solution.py:51
  470.5 4.7 constant_dynamic-slice_fusion.2
  475.3 5.4 copy.17
  480.6 4.4 fusion.4
  485.1 2.0 copy-done.2
  487.1 11.7 %cholesky.223 = f32[128,128]{1,0:T(8,128)S(1)} custom-call(f32[128,128]{1,0:T(8,128)S(1)} %cholesky.580), custom_call_target="Cholesky" | custom-call | tf_op jit(solution)/shard_map/jit(cholesky)/cholesky | solution.py:54
  498.8 2.5 cholesky.255
  501.3 9.8 %custom-call.62 = f32[1,128,128]{1,2,0:T(8,128)S(1)} custom-call(f32[1,128,128]{2,1,0:T(8,128)S(1)} %get-tuple-element.73), custom_call_target="InvertDiagBlocksLowerTriangular" | custom-call | tf_op jit(solution)/shard_map/jit(cholesky)/cholesky | solution.py:54
  511.1 2.4 constant_dynamic-update-slice_fusion.25
  513.5 1.5 convolution_subtract_fusion.6
  515.0 11.9 %cholesky.244 = f32[128,128]{1,0:T(8,128)S(1)} custom-call(f32[128,128]{1,0:T(8,128)S(1)} %cholesky.584), custom_call_target="Cholesky" | custom-call | tf_op jit(solution)/shard_map/jit(cholesky)/cholesky | solution.py:54
  527.5 9.8 %custom-call.63 = f32[1,128,128]{1,2,0:T(8,128)S(1)} custom-call(f32[1,128,128]{2,1,0:T(8,128)S(1)} %get-tuple-element.70), custom_call_target="InvertDiagBlocksLowerTriangular" | custom-call | tf_op jit(solution)/shard_map/jit(cholesky)/cholesky | solution.py:54
  538.6 2.1 convolution_subtract_fusion.7
  540.7 11.7 %cholesky.468 = f32[128,128]{1,0:T(8,128)S(1)} custom-call(f32[128,128]{1,0:T(8,128)S(1)} %cholesky.589), custom_call_target="Cholesky" | custom-call | tf_op jit(solution)/shard_map/jit(cholesky)/cholesky | solution.py:54
  553.1 9.8 %custom-call.64 = f32[1,128,128]{1,2,0:T(8,128)S(1)} custom-call(f32[1,128,128]{2,1,0:T(8,128)S(1)} %get-tuple-element.67), custom_call_target="InvertDiagBlocksLowerTriangular" | custom-call | tf_op jit(solution)/shard_map/jit(cholesky)/cholesky | solution.py:54
  564.1 2.3 convolution_subtract_fusion.8
  566.4 11.9 %cholesky.487 = f32[128,128]{1,0:T(8,128)S(1)} custom-call(f32[128,128]{1,0:T(8,128)S(1)} %cholesky.594), custom_call_target="Cholesky" | custom-call | tf_op jit(solution)/shard_map/jit(cholesky)/cholesky | solution.py:54
  579.0 9.8 %custom-call.65 = f32[1,128,128]{1,2,0:T(8,128)S(1)} custom-call(f32[1,128,128]{2,1,0:T(8,128)S(1)} %get-tuple-element.64), custom_call_target="InvertDiagBlocksLowerTriangular" | custom-call | tf_op jit(solution)/shard_map/jit(cholesky)/cholesky | solution.py:54
  589.9 2.3 convolution_subtract_fusion.9
  592.3 11.7 %cholesky.506 = f32[128,128]{1,0:T(8,128)S(1)} custom-call(f32[128,128]{1,0:T(8,128)S(1)} %cholesky.599), custom_call_target="Cholesky" | custom-call | tf_op jit(solution)/shard_map/jit(cholesky)/cholesky | solution.py:54
  604.6 10.2 %custom-call.66 = f32[1,128,128]{1,2,0:T(8,128)S(1)} custom-call(f32[1,128,128]{2,1,0:T(8,128)S(1)} %get-tuple-element.61), custom_call_target="InvertDiagBlocksLowerTriangular" | custom-call | tf_op jit(solution)/shard_map/jit(cholesky)/cholesky | solution.py:54
  615.8 2.3 convolution_subtract_fusion.10
  618.1 11.7 %cholesky.526 = f32[128,128]{1,0:T(8,128)S(1)} custom-call(f32[128,128]{1,0:T(8,128)S(1)} %cholesky.604), custom_call_target="Cholesky" | custom-call | tf_op jit(solution)/shard_map/jit(cholesky)/cholesky | solution.py:54
  630.5 9.8 %custom-call.67 = f32[1,128,128]{1,2,0:T(8,128)S(1)} custom-call(f32[1,128,128]{2,1,0:T(8,128)S(1)} %get-tuple-element.58), custom_call_target="InvertDiagBlocksLowerTriangular" | custom-call | tf_op jit(solution)/shard_map/jit(cholesky)/cholesky | solution.py:54
  641.2 2.0 convolution_subtract_fusion.11
  643.3 11.7 %cholesky.546 = f32[128,128]{1,0:T(8,128)S(1)} custom-call(f32[128,128]{1,0:T(8,128)S(1)} %cholesky.609), custom_call_target="Cholesky" | custom-call | tf_op jit(solution)/shard_map/jit(cholesky)/cholesky | solution.py:54
  655.6 9.8 %custom-call.68 = f32[1,128,128]{1,2,0:T(8,128)S(1)} custom-call(f32[1,128,128]{2,1,0:T(8,128)S(1)} %get-tuple-element.55), custom_call_target="InvertDiagBlocksLowerTriangular" | custom-call | tf_op jit(solution)/shard_map/jit(cholesky)/cholesky | solution.py:54
  666.3 1.8 convolution_subtract_fusion.12
  668.1 11.7 %cholesky.564 = f32[128,128]{1,0:T(8,128)S(1)} custom-call(f32[128,128]{1,0:T(8,128)S(1)} %convolution_subtract_fusion.12), custom_call_target="Cholesky" | custom-call | tf_op jit(solution)/shard_map/jit(cholesky)/cholesky | solution.py:54
  690.5 4.4 fusion.5
  694.9 22.9 %while.1 = (s32[]{:T(128)}, f32[1024,1024]{1,0:T(8,128)}, s32[8,2]{0,1:T(2,128)S(1)}, f32[8,128,128]{2,1,0:T(8,128)S(1)}, s32[]{:T(128)}) while((s32[]{:T(128)}, f32[1024,1024]{1,0:T(8,128)}, s32[8,2]{0,1:T(2,128)S(1)}, f32[8,128,128]{2,1,0:T(8,128)S(1)}, s32[]{:T(128)}) %tuple.58), condition=%wide.while_cond, body=%wide.while_body.sunk | while | flops 2 | bytes 131189 | solution.py:55
  695.6 2.2 bitcast_dynamic-update-slice_fusion.2
  698.4 2.2 bitcast_dynamic-update-slice_fusion.2
  701.3 2.2 bitcast_dynamic-update-slice_fusion.2
  704.2 2.2 bitcast_dynamic-update-slice_fusion.2
  707.1 2.2 bitcast_dynamic-update-slice_fusion.2
  709.9 2.2 bitcast_dynamic-update-slice_fusion.2
  712.8 2.2 bitcast_dynamic-update-slice_fusion.2
  715.7 2.2 bitcast_dynamic-update-slice_fusion.2
  717.8 78.8 %custom-call.69 = f32[8,128,128]{1,2,0:T(8,128)S(1)} custom-call(f32[8,128,128]{2,1,0:T(8,128)S(1)} %get-tuple-element.12), custom_call_target="InvertDiagBlocksLowerTriangular" | custom-call | tf_op jit(solution)/shard_map/triangular_solve | solution.py:55
  797.2 1.9 convolution_subtract_fusion.5
  799.9 1.6 convolution_subtract_fusion.1
  802.3 2.0 fusion.37
  805.1 2.2 fusion.40
  808.0 2.6 convolution_subtract_fusion.3
  811.4 2.8 convolution_subtract_fusion.2
  814.8 3.5 convolution_subtract_fusion.4
  821.4 55.3 %all-reduce.8.cloned.1.call-done = f32[256,1024]{1,0:T(8,128)} async-done(((f32[256,1024]{1,0:T(8,128)}), f32[256,1024]{1,0:T(8,128)}) %all-reduce.8.cloned.1.call-update) | async-done | bytes 1048592 | tf_op jit(solution)/shard_map/psum | solution.py:14
  876.9 17.0 %convolution_select_fusion = f32[2048,256]{1,0:T(8,128)} fusion(f32[2048,256]{1,0:T(8,128)S(1)} %bitcast.127, f32[2048,1024]{0,1:T(8,128)} %all-reduce.6.cloned.1.call-done, f32[256,1024]{1,0:T(8,128)} %all-reduce.8.cloned.1.call-done, pred[2048]{0:T(1024)(128)(4,1)S(1)} %fusion.93), kind=kOutput, calls=%fused_computation.17 | convolution fusion | flops 6442975232 | bytes 13633536 | tf_op jit(solution)/shard_map/dot_general | solution.py:60
  (76 shorter events, 33.4 us)
Async XLA Ops:
  6.5 129.8 %all-reduce.10.cloned.1.call-start = ((), (), s32[]{:S(2)}) async-start(), calls=%async_computation.2 | async-start | bytes 12582912 | tf_op jit(solution)/shard_map/psum | solution.py:14
  24.5 3.0 copy-start.1
  29.5 441.0 %all-reduce.6.cloned.1.call-start = ((), (), s32[]{:S(2)}) async-start(), calls=%async_computation | async-start | bytes 16777216 | tf_op jit(solution)/shard_map/psum | solution.py:51
  164.9 2.7 copy-start.3
  179.4 697.3 %all-reduce.8.cloned.1.call-start = ((), (), s32[]{:S(2)}) async-start(), calls=%async_computation.1 | async-start | bytes 2097152 | tf_op jit(solution)/shard_map/psum | solution.py:14
  485.1 2.0 copy-start.2
  796.7 3.2 copy-start
Sparse Core Ops, SparseCore 0:
  29.6 106.6 all-reduce.9
  179.6 290.9 all-reduce.5
  820.2 56.4 all-reduce.7
where the time goes:
time: 912 us; the launch traced here: 901 us
  waiting for transfers between devices  416 us (46%)
  other arithmetic  270 us (30%)
  local copies, waits for them, and re-layouts  103 us (11%)
  matrix products  90.7 us (10%)
  between operations  21.6 us (2%)
    psum x1, waiting for transfers between devices, local(): updated_tiles = lax.psum(placed - update_terms, 'col')  288 us
    another operation x31, other arithmetic, local(): cholesky_factor = jnp.linalg.cholesky(diagonal)  173 us
    psum x2, waiting for transfers between devices, from_root(): return lax.psum(kept, axis)  127 us
    another operation x3, other arithmetic, local(): lax.linalg.triangular_solve(cholesky_factor, identity, left_side=True, lo...  83.2 us
    another operation x14, matrix products, local(): cholesky_factor = jnp.linalg.cholesky(diagonal)  23.1 us
    another operation x24, local copies, waits for them, and re-layouts  22.7 us
    another operation x15, matrix products, local(): lax.linalg.triangular_solve(cholesky_factor, identity, left_side=True, lo...  22.2 us
  transfers between devices with their start and end apart: 3, of which 3 were waited for; matrix products, arithmetic and copies ran while one was open for 4% of the time, Pallas kernels for 0%

commit v1 on v0

--- a/solution.py
+++ b/solution.py
@@ -7,11 +7,14 @@
 RANK = 256
 TILE_DEV = 2
 COL_DEV = 6
+sums_all_store = lambda matrix, axis_tag: jnp.sum(
+    lax.all_gather(matrix, axis_name=axis_tag), axis=0
+)
 
 
 def from_root(value, axis, source):
     kept = jnp.where(lax.axis_index(axis) == source, value, 0).astype(value.dtype)
-    return lax.psum(kept, axis)
+    return sums_all_store(kept, axis)
 
 
 def local(panel_tiles, left_u, earlier_right_factors, tile_global_index):

time: 912 us -> 1060 us (1.16)
  waiting for transfers between devices: 416 us -> 541 us
  other arithmetic: 270 us -> 308 us
  local copies, waits for them, and re-layouts: 103 us -> 92 us
    all_gather x0 -> x3, waiting for transfers between devices: none -> 253 us  [lax.all_gather(matrix, axis_name=axis_tag)]
    psum x2 -> x0, waiting for transfers between devices: 127 us -> none  [from_root(): return lax.psum(kept, axis)]
    reduce_sum x0 -> x3, other arithmetic: none -> 34.7 us  [jnp.sum(lax.all_gather(matrix, axis_name=axis_tag), axis=0)]
    another operation x31 -> x30, other arithmetic: 173 us -> 172 us  [local(): cholesky_factor = jnp.linalg.cholesky(diagonal)]
  transfers between devices with their start and end apart: 3 -> 4, of which waited for: 3 -> 4; matrix products, arithmetic and copies ran while one was open for 4% -> 6% of each run, Pallas kernels for 0% -> 0%
where the time goes in v1:
time: 1060 us; the launch traced here: 1050 us
  waiting for transfers between devices  541 us (51%)
  other arithmetic  308 us (29%)
  local copies, waits for them, and re-layouts  92 us (9%)
  matrix products  89.5 us (8%)
  between operations  21.6 us (2%)
    psum x1, waiting for transfers between devices, local(): updated_tiles = lax.psum(placed - update_terms, 'col')  288 us
    all_gather x3, waiting for transfers between devices, lax.all_gather(matrix, axis_name=axis_tag)  253 us
    another operation x30, other arithmetic, local(): cholesky_factor = jnp.linalg.cholesky(diagonal)  172 us
    another operation x3, other arithmetic, local(): lax.linalg.triangular_solve(cholesky_factor, identity, left_side=True, lo...  83.3 us
    reduce_sum x3, other arithmetic, jnp.sum(lax.all_gather(matrix, axis_name=axis_tag), axis=0)  34.7 us
    another operation x24, local copies, waits for them, and re-layouts  23.4 us
    another operation x14, matrix products, local(): cholesky_factor = jnp.linalg.cholesky(diagonal)  23.1 us
    another operation x15, matrix products, local(): lax.linalg.triangular_solve(cholesky_factor, identity, left_side=True, lo...  22.2 us
  transfers between devices with their start and end apart: 4, of which 4 were waited for; matrix products, arithmetic and copies ran while one was open for 6% of the time, Pallas kernels for 0%

profile of v1, /device:TPU:0, one launch (start us, length us, event | category | flops | bytes accessed | tf_op | source)
XLA Modules:
  0.0 1052.3 jit_solution(16338224078925837357)
XLA Ops:
  10.7 4.1 dynamic-slice_select_fusion
  14.9 4.2 dynamic-slice_select_fusion.1
  19.2 13.7 %reshape.130 = bf16[2,1024,6,256]{3,2,1,0:T(8,128)(2,1)} reshape(bf16[2048,1536]{1,0:T(8,128)(2,1)} %param.5) | data formatting | bytes 12582912 | tf_op jit(solution)/shard_map/reshape | solution.py:36
  32.9 13.3 %reshape.129 = bf16[2,1024,6,256]{3,2,1,0:T(8,128)(2,1)} reshape(bf16[2048,1536]{1,0:T(8,128)(2,1)} %param.6) | data formatting | bytes 12582912 | tf_op jit(solution)/shard_map/reshape | solution.py:37
  46.2 1.9 copy.16
  48.1 4.2 broadcast_in_dim.26
  53.8 89.1 %all-gather.9.cloned.1.call-done = bf16[8192,1536]{1,0:T(8,128)(2,1)} async-done(((bf16[1024,1536]{1,0:T(8,128)(2,1)}), bf16[8192,1536]{1,0:T(8,128)(2,1)}) %all-gather.9.cloned.1.call-update) | async-done | bytes 25165840 | tf_op jit(solution)/shard_map/all_gather | solution.py:11
  142.9 16.5 %reduce_sum.44 = bf16[1024,1536]{1,0:T(8,128)(2,1)} reduce(bf16[8,1024,1536]{2,1,0:T(8,128)(2,1)} %bitcast.124, bf16[]{:T(256)} %constant.325.clone.1), dimensions={0}, to_apply=%region_2.3 | reduce | flops 11010048 | bytes 28311554 | tf_op jit(solution)/shard_map/reduce_sum | solution.py:10
  159.4 110.6 %all-gather.7.cloned.1.call-done = bf16[8192,1536]{1,0:T(8,128)(2,1)} async-done(((bf16[1024,1536]{1,0:T(8,128)(2,1)}), bf16[8192,1536]{1,0:T(8,128)(2,1)}) %all-gather.7.cloned.1.call-update) | async-done | bytes 25165840 | tf_op jit(solution)/shard_map/all_gather | solution.py:11
  270.0 13.8 %reduce_sum.43 = bf16[1024,1536]{1,0:T(8,128)(2,1)S(1)} reduce(bf16[8,1024,1536]{2,1,0:T(8,128)(2,1)} %bitcast.125, bf16[]{:T(256)} %constant.325.clone.1), dimensions={0}, to_apply=%region_1.2 | reduce | flops 11010048 | bytes 28311554 | tf_op jit(solution)/shard_map/reduce_sum | solution.py:10
  283.8 3.0 copy.17
  286.8 16.6 %convert_bitcast_fusion = bf16[2,1024,6,256]{1,3,2,0:T(8,128)(2,1)} fusion(bf16[2,1024,6,256]{3,2,1,0:T(8,128)(2,1)} %reshape.130, bf16[1024,6,256,1]{0,2,1,3:T(8,128)(2,1)} %bitcast.129, bf16[2,1024,6,256]{3,2,1,0:T(8,128)(2,1)} %reshape.129), kind=kOutput, calls=%fused_computation.6 | convolution fusion | flops 3225157632 | bytes 22020096 | tf_op jit(solution)/shard_map/tbjr,tjrs->tbjs/dot_general | solution.py:42
  303.4 12.3 %copy.22 = bf16[2,1024,6,256]{1,0,3,2:T(2,128)(2,1)S(1)} copy(bf16[2,1024,6,256]{1,3,2,0:T(8,128)(2,1)} %convert_bitcast_fusion) | data formatting | bytes 12582912 | tf_op jit(solution)/shard_map/convert_element_type | solution.py:44
  315.7 2.7 copy.30
  318.3 11.0 %convolution_subtract_fusion = f32[2048,1024]{0,1:T(8,128)} fusion(f32[2048,1024]{0,1:T(8,128)} %constant_dynamic-update-slice_fusion.26, bf16[1024,1536]{1,0:T(8,128)(2,1)S(1)} %copy-done.2, bf16[2048,1536]{0,1:T(8,128)(2,1)S(1)} %bitcast.128), kind=kOutput, calls=%fused_computation.13 | convolution fusion | flops 6444548096 | bytes 26214400 | tf_op jit(solution)/shard_map/nk,mk->nm/dot_general | solution.py:45
  329.8 2.4 fusion.36
  332.2 288.1 %all-reduce.3.cloned.1.call-done = f32[2048,1024]{0,1:T(8,128)} async-done(((f32[2048,1024]{0,1:T(8,128)}), f32[2048,1024]{0,1:T(8,128)}) %all-reduce.3.cloned.1.call-update) | async-done | bytes 8388624 | tf_op jit(solution)/shard_map/psum | solution.py:54
  620.3 4.7 constant_dynamic-slice_fusion.2
  625.1 5.4 copy.24
  630.5 4.4 fusion.4
  634.9 2.0 copy-done.1
  636.9 11.7 %cholesky.223 = f32[128,128]{1,0:T(8,128)S(1)} custom-call(f32[128,128]{1,0:T(8,128)S(1)} %cholesky.580), custom_call_target="Cholesky" | custom-call | tf_op jit(solution)/shard_map/jit(cholesky)/cholesky | solution.py:57
  648.6 2.5 cholesky.255
  651.1 9.8 custom-call.62
  660.9 2.4 constant_dynamic-update-slice_fusion.25
  664.9 11.9 %cholesky.244 = f32[128,128]{1,0:T(8,128)S(1)} custom-call(f32[128,128]{1,0:T(8,128)S(1)} %cholesky.584), custom_call_target="Cholesky" | custom-call | tf_op jit(solution)/shard_map/jit(cholesky)/cholesky | solution.py:57
  677.4 9.8 custom-call.63
  688.5 2.1 convolution_subtract_fusion.7
  690.6 11.7 %cholesky.468 = f32[128,128]{1,0:T(8,128)S(1)} custom-call(f32[128,128]{1,0:T(8,128)S(1)} %cholesky.589), custom_call_target="Cholesky" | custom-call | tf_op jit(solution)/shard_map/jit(cholesky)/cholesky | solution.py:57
  702.9 9.8 custom-call.64
  713.9 2.3 convolution_subtract_fusion.8
  716.3 11.9 %cholesky.487 = f32[128,128]{1,0:T(8,128)S(1)} custom-call(f32[128,128]{1,0:T(8,128)S(1)} %cholesky.594), custom_call_target="Cholesky" | custom-call | tf_op jit(solution)/shard_map/jit(cholesky)/cholesky | solution.py:57
  728.9 9.8 custom-call.65
  739.8 2.3 convolution_subtract_fusion.9
  742.1 11.7 %cholesky.506 = f32[128,128]{1,0:T(8,128)S(1)} custom-call(f32[128,128]{1,0:T(8,128)S(1)} %cholesky.599), custom_call_target="Cholesky" | custom-call | tf_op jit(solution)/shard_map/jit(cholesky)/cholesky | solution.py:57
  754.5 10.2 custom-call.66
  765.7 2.3 convolution_subtract_fusion.10
  768.0 11.7 %cholesky.526 = f32[128,128]{1,0:T(8,128)S(1)} custom-call(f32[128,128]{1,0:T(8,128)S(1)} %cholesky.604), custom_call_target="Cholesky" | custom-call | tf_op jit(solution)/shard_map/jit(cholesky)/cholesky | solution.py:57
  780.3 9.8 custom-call.67
  791.1 2.0 convolution_subtract_fusion.11
  793.1 11.7 %cholesky.546 = f32[128,128]{1,0:T(8,128)S(1)} custom-call(f32[128,128]{1,0:T(8,128)S(1)} %cholesky.609), custom_call_target="Cholesky" | custom-call | tf_op jit(solution)/shard_map/jit(cholesky)/cholesky | solution.py:57
  805.5 9.8 custom-call.68
  816.1 1.8 convolution_subtract_fusion.12
  817.9 11.7 %cholesky.564 = f32[128,128]{1,0:T(8,128)S(1)} custom-call(f32[128,128]{1,0:T(8,128)S(1)} %convolution_subtract_fusion.12), custom_call_target="Cholesky" | custom-call | tf_op jit(solution)/shard_map/jit(cholesky)/cholesky | solution.py:57
  839.7 4.5 fusion.5
  844.2 23.6 %while.1 = (s32[]{:T(128)}, f32[1024,1024]{1,0:T(8,128)}, s32[8,2]{0,1:T(2,128)S(1)}, f32[8,128,128]{2,1,0:T(8,128)S(1)}, s32[]{:T(128)}) while((s32[]{:T(128)}, f32[1024,1024]{1,0:T(8,128)}, s32[8,2]{0,1:T(2,128)S(1)}, f32[8,128,128]{2,1,0:T(8,128)S(1)}, s32[]{:T(128)}) %tuple.58), condition=%wide.while_cond, body=%wide.while_body.sunk | while | flops 2 | bytes 131189 | solution.py:58
  844.8 2.3 bitcast_dynamic-update-slice_fusion.2
  847.8 2.3 bitcast_dynamic-update-slice_fusion.2
  850.7 2.3 bitcast_dynamic-update-slice_fusion.2
  853.7 2.3 bitcast_dynamic-update-slice_fusion.2
  856.6 2.3 bitcast_dynamic-update-slice_fusion.2
  859.6 2.3 bitcast_dynamic-update-slice_fusion.2
  862.5 2.3 bitcast_dynamic-update-slice_fusion.2
  865.5 2.2 bitcast_dynamic-update-slice_fusion.2
  867.7 78.8 %custom-call.69 = f32[8,128,128]{1,2,0:T(8,128)S(1)} custom-call(f32[8,128,128]{2,1,0:T(8,128)S(1)} %get-tuple-element.12), custom_call_target="InvertDiagBlocksLowerTriangular" | custom-call | tf_op jit(solution)/shard_map/triangular_solve | solution.py:58
  947.1 1.9 convolution_subtract_fusion.5
  952.2 2.0 fusion.30
  954.9 2.2 fusion.33
  957.9 2.6 convolution_subtract_fusion.3
  961.2 2.8 convolution_subtract_fusion.2
  964.7 3.5 convolution_subtract_fusion.4
  971.2 52.9 %all-gather.11.cloned.1.call-done = f32[2048,1024]{1,0:T(8,128)} async-done(((f32[256,1024]{1,0:T(8,128)}), f32[2048,1024]{1,0:T(8,128)}) %all-gather.11.cloned.1.call-update) | async-done | bytes 8388624 | tf_op jit(solution)/shard_map/all_gather | solution.py:11
  1024.1 4.4 reduce_sum.45
  1028.7 16.7 %convolution_select_fusion = f32[2048,256]{1,0:T(8,128)} fusion(f32[2048,256]{1,0:T(8,128)S(1)} %bitcast.126, f32[2048,1024]{0,1:T(8,128)} %all-reduce.3.cloned.1.call-done, f32[256,1024]{1,0:T(8,128)S(1)} %reduce_sum.45, pred[2048]{0:T(1024)(128)(4,1)S(1)} %fusion.86), kind=kOutput, calls=%fused_computation.16 | convolution fusion | flops 6442975232 | bytes 13633536 | tf_op jit(solution)/shard_map/dot_general | solution.py:63
  (77 shorter events, 35.1 us)
Async XLA Ops:
  6.5 136.4 %all-gather.9.cloned.1.call-start = ((), (), s32[]{:S(2)}) async-start(), calls=%async_computation.2 | async-start | bytes 28311552 | tf_op jit(solution)/shard_map/all_gather | solution.py:11
  14.8 255.2 %all-gather.7.cloned.1.call-start = ((), (), s32[]{:S(2)}) async-start(), calls=%async_computation.1 | async-start | bytes 28311552 | tf_op jit(solution)/shard_map/all_gather | solution.py:11
  19.1 601.2 %all-reduce.3.cloned.1.call-start = ((), (), s32[]{:S(2)}) async-start(), calls=%async_computation | async-start | bytes 16777216 | tf_op jit(solution)/shard_map/psum | solution.py:54
  315.6 2.7 copy-start.2
  329.4 694.8 %all-gather.11.cloned.1.call-start = ((), (), s32[]{:S(2)}) async-start(), calls=%async_computation.3 | async-start | bytes 9437184 | tf_op jit(solution)/shard_map/all_gather | solution.py:11
  634.9 2.0 copy-start.1
  946.5 3.2 copy-start
Sparse Core Ops, SparseCore 0:
  14.9 127.9 all-gather.8
  144.8 125.1 all-gather.6
  329.5 290.8 all-reduce.2
  970.1 54.0 all-gather.10
